TPU v7x, 32 devices: a whole 2x2x4 slice. The times are simulated.
32 devices in a mesh: mem: 4 (over y, core), lat: 2 (over x), lon: 4 (over z).
Axes of the slice: x: 2, y: 2, z: 4, core: 2. Of those that a mesh axis runs over, the one named last changes fastest.
Arguments:
- perturbations: bfloat16 [8, 4, 768, 1536], P('mem', None, 'lat', 'lon'), may hold values from -2 to 2
- innovation: float32 [2, 8192], P('lat', 'lon'), may hold values from -4.2 to 4.2
- obs_weight: float32 [2, 8192], P('lat', 'lon'), may hold values from 0.5 to 6, as said below
- obs_cell: int32 [2, 8192], P('lat', 'lon'), may hold values from 0 to 147455
- obs_level: int32 [2, 8192], P('lat', 'lon'), may hold values from 0 to 3
- cutoff: int32 [4], replicated, may hold values from 16 to 127
Outputs:
- solution: float32 [8, 4, 768, 512], P('mem', None, ('lat', 'lon'))
- residual: float32 [8, 4, 768, 512], P('mem', None, ('lat', 'lon'))
Inputs may be any that keep to these rules, and one draw needn't show every extreme that they name: `obs_weight`: positive weights.
All inputs are finite; a program needn't handle non-finite values.
Results may differ from a plain program's by a relative error of at most 0.0008.
Values may be sent and summed in bfloat16 or wider, within the bound.
No kernel may reach another device: no remote copies, remote signals or barrier semaphores. Data moves between devices by JAX's collectives and lax.ppermute only.
A program may use at most 64 MiB of HBM per device.

v0:
```python
import jax
import jax.numpy as jnp
from jax import lax
from jax.sharding import PartitionSpec as P

NLON = 1536
KMAX = 256
ITERS = 2


def basis_table(transposed):
    factor = 2.0 * jnp.pi / NLON
    if transposed:
        columns = jnp.arange(NLON, dtype=jnp.int32)[None, :]
        cos_waves = jnp.arange(KMAX, dtype=jnp.int32)[:, None]
        axis_join = 0
    else:
        columns = jnp.arange(NLON, dtype=jnp.int32)[:, None]
        cos_waves = jnp.arange(KMAX, dtype=jnp.int32)[None, :]
        axis_join = 1
    cos_phase = (columns * cos_waves % NLON).astype(jnp.float32) * factor
    sin_phase = (columns * (cos_waves + 1) % NLON).astype(jnp.float32) * factor
    joined = jnp.concatenate([jnp.cos(cos_phase), jnp.sin(sin_phase)], axis=axis_join)
    return joined / jnp.sqrt(jnp.float32(KMAX))


def spectrum_of(cutoff):
    wavenumbers = jnp.concatenate(
        [jnp.arange(KMAX, dtype=jnp.float32), jnp.arange(1, KMAX + 1, dtype=jnp.float32)]
    )
    scaled = wavenumbers[None, :] / cutoff.astype(jnp.float32)[:, None]
    return 1.0 / (1.0 + scaled * scaled)


def member_total(partial_value):
    return lax.psum(partial_value, "mem")


def norm_total(residual):
    return lax.psum(jnp.sum(residual * residual), ("mem", "lat", "lon"))


def body(perturbations, innovation, obs_weight, obs_cell, obs_level, cutoff):
    members_here, levels, tile_rows, tile_cols = perturbations.shape
    line_rows = tile_rows // lax.axis_size("lon")
    basis_rows = basis_table(False)
    basis_cols = basis_table(True)
    spectrum = spectrum_of(cutoff)
    located = (obs_level * (tile_rows * tile_cols) + obs_cell).reshape(-1)
    weights = obs_weight.reshape(-1)

    def gridded_of(weighted):
        field = jnp.zeros((levels * tile_rows * tile_cols,), jnp.float32).at[located].add(weighted)
        return field.reshape(levels, tile_rows, tile_cols)

    def analyse(products):
        summed = jnp.dot(
            products.reshape(-1, NLON),
            basis_rows,
            precision=lax.Precision.HIGHEST,
            preferred_element_type=jnp.float32,
        )
        return (
            summed.reshape(members_here, levels, line_rows, 2 * KMAX) * spectrum[None, :, None, :]
        )

    line_pert = lax.all_to_all(perturbations, "lon", split_axis=2, concat_axis=3, tiled=True)

    def adjoint_part(gridded):
        grid_lines = lax.all_to_all(gridded, "lon", split_axis=1, concat_axis=2, tiled=True)
        products = line_pert.astype(jnp.float32) * grid_lines[None]
        return analyse(products)

    right_side = adjoint_part(gridded_of(weights * innovation.reshape(-1)))
    solution = jnp.zeros_like(right_side)
    residual = right_side
    direction = right_side
    norm_now = norm_total(residual)
    for iteration in range(ITERS):
        coeffs = direction * spectrum[None, :, None, :]
        synthesized = jnp.dot(
            coeffs.reshape(-1, 2 * KMAX),
            basis_cols,
            precision=lax.Precision.HIGHEST,
            preferred_element_type=jnp.float32,
        )
        forward_synthesized = synthesized.reshape(members_here, levels, line_rows, NLON)
        partial_value = jnp.sum(line_pert.astype(jnp.float32) * forward_synthesized, axis=0)
        on_tiles = lax.all_to_all(partial_value, "lon", split_axis=2, concat_axis=1, tiled=True)
        increment = member_total(on_tiles)
        sampled = increment.reshape(-1)[located]
        image = direction + adjoint_part(gridded_of(weights * sampled))
        curvature = lax.psum(jnp.sum(direction * image), ("mem", "lat", "lon"))
        step_size = norm_now / curvature
        solution = solution + step_size * direction
        residual = residual - step_size * image
        if iteration + 1 < ITERS:
            norm_next = norm_total(residual)
            direction = residual + norm_next / norm_now * direction
            norm_now = norm_next
    return (solution, residual)


def solution(mesh):
    placed = (
        P("mem", None, "lat", "lon"),
        P("lat", "lon"),
        P("lat", "lon"),
        P("lat", "lon"),
        P("lat", "lon"),
        P(),
    )
    return jax.shard_map(
        body,
        mesh=mesh,
        in_specs=placed,
        out_specs=(P("mem", None, ("lat", "lon"), None), P("mem", None, ("lat", "lon"), None)),
        check_vma=False,
    )
```

profile of v0, /device:TPU:0, one launch (start us, length us, event | category | flops | bytes accessed | tf_op | source)
XLA Modules:
  0.0 842.8 jit_solution(17484831876931123835)
XLA Ops:
  8.6 12.8 %scatter_custom_fusion = f32[589824]{0:T(1024)} fusion(s32[2048]{0:T(1024)S(1)} %bitcast.74, f32[2048]{0:T(1024)S(1)} %mul.200, f32[]{:T(128)} %constant.20.clone.1), kind=kCustom, calls=%fused_computation.75 | custom fusion | flops 2048 | bytes 2359300 | tf_op jit(solution)/shard_map/scatter-add | solution.py:53
  24.8 4.6 copy.45
  29.4 6.3 all-to-all-start.1
  35.7 4.9 copy.43
  40.6 49.0 %all-to-all-done.1 = f32[4,384,384]{2,0,1:T(4,128)} async-done(((f32[4,384,384]{2,0,1:T(4,128)}), f32[4,384,384]{2,0,1:T(4,128)}, u32[]{:S(2)}, u32[]{:S(2)}) %all-to-all-start.1) | async-done | bytes 2359328 | tf_op jit(solution)/shard_map/all_to_all | solution.py:70
  94.5 5.9 fusion.18
  100.4 8.1 fusion.24
  108.5 6.8 fusion.21
  115.3 7.0 fusion.27
  125.9 21.6 %all-to-all-done = bf16[2,4,384,384]{3,1,0,2:T(4,128)(2,1)} async-done(((bf16[2,4,384,384]{3,1,0,2:T(4,128)(2,1)}), bf16[2,4,384,384]{3,1,0,2:T(4,128)(2,1)}, u32[]{:S(2)}, u32[]{:S(2)}) %all-to-all-start) | async-done | bytes 2359328 | tf_op jit(solution)/shard_map/all_to_all | solution.py:67
  147.6 5.7 copy.70
  153.3 6.4 reshape.141
  159.6 10.9 %fusion.47 = f32[2,4,96,512]{3,2,1,0:T(8,128)S(1)} fusion(f32[1536,256]{1,0:T(8,128)} %fusion.21, f32[1536,256]{1,0:T(8,128)S(1)} %fusion.18, f32[2,4,96,1536]{3,2,1,0:T(8,128)} %reshape.141, f32[4,96,1536]{2,1,0:T(8,128)} %bitcast.63, f32[4,512]{1,0:T(4,128)S(1)} %fusion.65), kind=kOutput, calls=%fused_computation.70 | convolution fusion | flops 7250903040 | bytes 11804672 | tf_op jit(solution)/shard_map/dot_general | solution.py:57
  170.6 10.3 %multiply_reduce_fusion.1 = f32[4,96,1536]{2,1,0:T(8,128)} fusion(f32[2,4,96,1536]{3,2,1,0:T(8,128)S(1)} %copy-done, f32[256,1536]{1,0:T(8,128)S(1)} %copy-done.10, f32[256,1536]{1,0:T(8,128)S(1)} %copy-done.8, f32[2,4,96,512]{3,2,1,0:T(8,128)S(1)} %fusion.47, f32[4,512]{1,0:T(4,128)S(1)} %fusion.65), kind=kOutput, calls=%fused_computation.11 | convolution fusion | flops 7251492864 | bytes 11804672 | tf_op jit(solution)/shard_map/dot_general | solution.py:81
  185.4 75.5 %all_to_all.90 = f32[4,96,1536]{1,0,2:T(4,128)} all-to-all(f32[4,96,1536]{1,0,2:T(4,128)} %copy.48), channel_id=1, replica_groups=mesh['mem'=4,'lat'=2,'lon'=4] {'lon'}, dimensions={2} | all-to-all | bytes 4718592 | tf_op jit(solution)/shard_map/all_to_all | solution.py:89
  261.0 4.7 copy.50
  269.0 54.8 %all-reduce.4.cloned.1.call-done = f32[589824]{0:T(1024)} async-done(((f32[589824]{0:T(1024)}), f32[589824]{0:T(1024)}) %all-reduce.4.cloned.1.call-update) | async-done | bytes 2359312 | tf_op jit(solution)/shard_map/psum | solution.py:36
  323.8 24.5 %gather_fusion = f32[2048]{0:T(1024)S(1)} fusion(f32[589824]{0:T(1024)} %all-reduce.4.cloned.1.call-done, s32[2048]{0:T(1024)S(1)} %broadcast_clamp_fusion), kind=kCustom, calls=%fused_computation | custom fusion | bytes 24576 | tf_op jit(solution)/shard_map/gather | solution.py:91
  348.3 12.8 %scatter_custom_fusion.1 = f32[589824]{0:T(1024)} fusion(s32[2048]{0:T(1024)S(1)} %bitcast.76, f32[2048]{0:T(1024)S(1)} %mul.226, f32[]{:T(128)} %constant.20.clone.1), kind=kCustom, calls=%fused_computation.73 | custom fusion | flops 2048 | bytes 2359300 | tf_op jit(solution)/shard_map/scatter-add | solution.py:53
  367.7 58.7 %all_to_all.91 = f32[4,384,384]{2,0,1:T(4,128)S(1)} all-to-all(f32[4,384,384]{2,0,1:T(4,128)S(1)} %copy.51), channel_id=1, replica_groups=mesh['mem'=4,'lat'=2,'lon'=4] {'lon'}, dimensions={1} | all-to-all | bytes 4718592 | tf_op jit(solution)/shard_map/all_to_all | solution.py:70
  428.5 8.6 %multiply_reduce_fusion.4 = (f32[]{:T(128)}, f32[]{:T(128)}, f32[2,4,96,512]{3,2,1,0:T(8,128)S(1)}) fusion(f32[2,4,96,512]{3,2,1,0:T(8,128)S(1)} %fusion.47, f32[4,512]{1,0:T(4,128)S(1)} %fusion.65, f32[1536,256]{1,0:T(8,128)S(1)} %copy-done.4, f32[1536,256]{1,0:T(8,128)S(1)} %copy-done.2, f32[2,4,96,1536]{3,2,1,0:T(8,128)S(1)} %bitcast.59, ...), kind=kOutput, calls=%fused_computation.45 | convolution fusion | flops 7252869120 | bytes 13377544 | tf_op jit(solution)/shard_map/dot_general | solution.py:57
  437.1 38.3 %all-reduce = (f32[]{:T(128)}, f32[]{:T(128)}) all-reduce(f32[]{:T(128)} %get-tuple-element.3, f32[]{:T(128)} %get-tuple-element.2), channel_id=1, replica_groups=mesh['mem'=4,'lat'=2,'lon'=4] {'mem','lat','lon'}, use_global_device_ids=true, to_apply=%region_2.3 | all-reduce | flops 2 | bytes 16 | tf_op jit(solution)/shard_map/psum | solution.py:40
  477.9 41.6 %psum.45 = f32[]{:T(128)} all-reduce(f32[]{:T(128)} %multiply_reduce_fusion.3), channel_id=1, replica_groups=mesh['mem'=4,'lat'=2,'lon'=4] {'mem','lat','lon'}, use_global_device_ids=true, to_apply=%region_9.10 | all-reduce | flops 1 | bytes 8 | tf_op jit(solution)/shard_map/psum | solution.py:40
  523.2 11.4 %multiply_reduce_fusion = f32[4,96,1536]{2,1,0:T(8,128)} fusion(f32[2,4,96,1536]{3,2,1,0:T(8,128)} %reshape.141, f32[256,1536]{1,0:T(8,128)S(1)} %copy-done.11, f32[256,1536]{1,0:T(8,128)S(1)} %copy-done.9, f32[2,4,96,512]{3,2,1,0:T(8,128)S(1)} %multiply_add_fusion.2, f32[4,512]{1,0:T(4,128)S(1)} %fusion.65), kind=kOutput, calls=%fused_computation.8 | convolution fusion | flops 7251492864 | bytes 11804672 | tf_op jit(solution)/shard_map/dot_general | solution.py:81
  539.1 75.7 %all_to_all.92 = f32[4,96,1536]{1,0,2:T(4,128)} all-to-all(f32[4,96,1536]{1,0,2:T(4,128)} %copy.54), channel_id=1, replica_groups=mesh['mem'=4,'lat'=2,'lon'=4] {'lon'}, dimensions={2} | all-to-all | bytes 4718592 | tf_op jit(solution)/shard_map/all_to_all | solution.py:89
  614.8 4.6 copy.56
  622.7 54.8 %all-reduce.6.cloned.1.call-done = f32[589824]{0:T(1024)} async-done(((f32[589824]{0:T(1024)}), f32[589824]{0:T(1024)}) %all-reduce.6.cloned.1.call-update) | async-done | bytes 2359312 | tf_op jit(solution)/shard_map/psum | solution.py:36
  677.4 24.5 %gather_fusion.1 = f32[2048]{0:T(1024)S(1)} fusion(f32[589824]{0:T(1024)} %all-reduce.6.cloned.1.call-done, s32[2048]{0:T(1024)S(1)} %broadcast_clamp_fusion), kind=kCustom, calls=%fused_computation.1 | custom fusion | bytes 24576 | tf_op jit(solution)/shard_map/gather | solution.py:91
  701.9 12.8 %scatter_custom_fusion.2 = f32[589824]{0:T(1024)} fusion(s32[2048]{0:T(1024)S(1)} %bitcast.77, f32[2048]{0:T(1024)S(1)} %mul.240, f32[]{:T(128)} %constant.20.clone.1), kind=kCustom, calls=%fused_computation.71 | custom fusion | flops 2048 | bytes 2359300 | tf_op jit(solution)/shard_map/scatter-add | solution.py:53
  721.3 58.4 %all_to_all.93 = f32[4,384,384]{2,0,1:T(4,128)S(1)} all-to-all(f32[4,384,384]{2,0,1:T(4,128)S(1)} %copy.57), channel_id=1, replica_groups=mesh['mem'=4,'lat'=2,'lon'=4] {'lon'}, dimensions={1} | all-to-all | bytes 4718592 | tf_op jit(solution)/shard_map/all_to_all | solution.py:70
  782.3 9.5 %multiply_reduce_fusion.2 = (f32[]{:T(128)}, f32[2,4,96,512]{3,2,1,0:T(8,128)}) fusion(f32[2,4,96,512]{3,2,1,0:T(8,128)S(1)} %copy-done.7, f32[4,512]{1,0:T(4,128)S(1)} %fusion.65, f32[1536,256]{1,0:T(8,128)S(1)} %copy-done.5, f32[1536,256]{1,0:T(8,128)S(1)} %copy-done.3, f32[2,4,96,1536]{3,2,1,0:T(8,128)S(1)} %bitcast.61, f32[4,96,1536]{2,1,0:T(8,128)S(1)} %bitcast.64), kind=kOutput, calls=%fused_computation.39 | convolution fusion | flops 7252082688 | bytes 13377540 | tf_op jit(solution)/shard_map/dot_general | solution.py:57
  791.8 38.3 %psum.47 = f32[]{:T(128)} all-reduce(f32[]{:T(128)} %get-tuple-element.9), channel_id=1, replica_groups=mesh['mem'=4,'lat'=2,'lon'=4] {'mem','lat','lon'}, use_global_device_ids=true, to_apply=%region_14.15 | all-reduce | flops 1 | bytes 8 | tf_op jit(solution)/shard_map/psum | solution.py:93
  (72 shorter events, 54.4 us)
Async XLA Ops:
  29.4 60.3 %all-to-all-start.1 = ((f32[4,384,384]{2,0,1:T(4,128)}), f32[4,384,384]{2,0,1:T(4,128)}, u32[]{:S(2)}, u32[]{:S(2)}) async-start(f32[4,384,384]{2,0,1:T(4,128)} %copy.45), calls=%async_computation.1 | async-start | bytes 4718592 | tf_op jit(solution)/shard_map/all_to_all | solution.py:70
  40.6 53.8 %copy-start.13 = (s32[4]{0:T(128)S(1)}, s32[4]{0:T(128)}, u32[]{:S(2)}) copy-start(s32[4]{0:T(128)} %param.11) | copy-start | bytes 52
  89.6 57.9 %all-to-all-start = ((bf16[2,4,384,384]{3,1,0,2:T(4,128)(2,1)}), bf16[2,4,384,384]{3,1,0,2:T(4,128)(2,1)}, u32[]{:S(2)}, u32[]{:S(2)}) async-start(bf16[2,4,384,384]{3,1,0,2:T(4,128)(2,1)} %copy.43), calls=%async_computation | async-start | bytes 4718592 | tf_op jit(solution)/shard_map/all_to_all | solution.py:67
  94.1 229.7 %all-reduce.4.cloned.1.call-start = ((), (), s32[]{:S(2)}) async-start(), calls=%async_computation.6 | async-start | bytes 4718592 | tf_op jit(solution)/shard_map/psum | solution.py:36
  100.4 59.2 %copy-start.1 = (f32[1536,256]{1,0:T(8,128)}, f32[1536,256]{1,0:T(8,128)S(1)}, u32[]{:S(2)}) copy-start(f32[1536,256]{1,0:T(8,128)S(1)} %fusion.18) | copy-start | bytes 4718596
  159.6 10.9 %copy-start = (f32[2,4,96,1536]{3,2,1,0:T(8,128)S(1)}, f32[2,4,96,1536]{3,2,1,0:T(8,128)}, u32[]{:S(2)}) copy-start(f32[2,4,96,1536]{3,2,1,0:T(8,128)} %reshape.141) | copy-start | bytes 14155780
  159.6 10.9 %copy-start.8 = (f32[256,1536]{1,0:T(8,128)S(1)}, f32[256,1536]{1,0:T(8,128)}, u32[]{:S(2)}) copy-start(f32[256,1536]{1,0:T(8,128)} %fusion.24) | copy-start | bytes 4718596
  159.6 11.0 %copy-start.10 = (f32[256,1536]{1,0:T(8,128)S(1)}, f32[256,1536]{1,0:T(8,128)}, u32[]{:S(2)}) copy-start(f32[256,1536]{1,0:T(8,128)} %fusion.27) | copy-start | bytes 4718596
  268.9 408.5 %all-reduce.6.cloned.1.call-start = ((), (), s32[]{:S(2)}) async-start(), calls=%async_computation.7 | async-start | bytes 4718592 | tf_op jit(solution)/shard_map/psum | solution.py:36
  268.9 79.3 %copy-start.12 = (f32[1,2048]{1,0:T(1,128)S(1)}, f32[1,2048]{1,0:T(1,128)}, u32[]{:S(2)}) copy-start(f32[1,2048]{1,0:T(1,128)} %param.8) | copy-start | bytes 24580
  367.7 59.2 %slice-start = ((s8[4718592]{0:T(1024)(128)(4,1)}), s8[4194304]{0:T(1024)(128)(4,1)S(1)}, s32[]{:S(2)}) async-start(s8[4718592]{0:T(1024)(128)(4,1)} %bitcast.58), calls=%async_computation.8 | async-start | bytes 8388608
  426.4 1.0 slice-start.1
  426.6 1.4 copy-start.2
  426.6 1.9 copy-start.4
  520.8 1.6 copy-start.9
  520.8 2.4 copy-start.11
  521.2 1.2 copy-start.6
  721.3 59.0 %slice-start.2 = ((s8[4718592]{0:T(1024)(128)(4,1)}), s8[4194304]{0:T(1024)(128)(4,1)S(1)}, s32[]{:S(2)}) async-start(s8[4718592]{0:T(1024)(128)(4,1)} %bitcast.60), calls=%async_computation.10 | async-start | bytes 8388608
  779.7 1.0 slice-start.3
  779.9 1.4 copy-start.3
  779.9 1.9 copy-start.5
  779.9 2.4 copy-start.7
Sparse Core Ops, SparseCore 0:
  269.0 54.7 all-reduce.3
  622.8 54.5 all-reduce.5
where the time goes:
time: 851 us; the launch traced here: 843 us
  blocking collectives  387 us (45%)
  waiting for transfers between devices  180 us (21%)
  local copies, waits for them, and re-layouts  122 us (14%)
  other arithmetic  73.6 us (9%)
  matrix products  50.7 us (6%)
  between operations  18.6 us (2%)
  starting transfers between devices  11.1 us (1%)
    all_to_all x2, blocking collectives, body(): lax.all_to_all(partial_value, 'lon', split_axis=2, concat_axis=1, tiled=T...  151 us
    all_to_all x2, blocking collectives, adjoint_part(): lax.all_to_all(gridded, 'lon', split_axis=1, concat_axis=2, tiled=True)  117 us
    psum x2, waiting for transfers between devices, member_total(): return lax.psum(partial_value, 'mem')  110 us
    psum x2, blocking collectives, norm_total(): return lax.psum(jnp.sum(residual * residual), ('mem', 'lat', 'lon'))  79.9 us
    all_to_all x1, waiting for transfers between devices, adjoint_part(): lax.all_to_all(gridded, 'lon', split_axis=1, concat_axis=2, tiled=True)  49 us
    gather x2, local copies, waits for them, and re-layouts, body(): sampled = increment.reshape(-1)[located]  49 us
    scatter-add x3, other arithmetic, gridded_of(): jnp.zeros((levels * tile_rows * tile_cols,), jnp.float32).at[located]  38.4 us
    psum x1, blocking collectives, body(): curvature = lax.psum(jnp.sum(direction * image), ('mem', 'lat', 'lon'))  38.3 us
  transfers between devices with their start and end apart: 4, of which 4 were waited for; matrix products, arithmetic and copies ran while one was open for 4% of the time, Pallas kernels for 0%

commit v1 on v0

--- a/solution.py
+++ b/solution.py
@@ -33,7 +33,7 @@
 
 
 def member_total(partial_value):
-    return lax.psum(partial_value, "mem")
+    return jnp.sum(lax.all_gather(partial_value, "mem"), axis=0)
 
 
 def norm_total(residual):

time: 851 us -> 881 us (1.035)
  waiting for transfers between devices: 180 us -> 197 us
  other arithmetic: 73.6 us -> 85.5 us
    all_gather x0 -> x2, waiting for transfers between devices: none -> 127 us  [member_total(): return jnp.sum(lax.all_gather(partial_value, 'mem'), axis=0)]
    psum x2 -> x0, waiting for transfers between devices: 110 us -> none  [member_total(): return lax.psum(partial_value, 'mem')]
    reduce_sum x0 -> x2, other arithmetic: none -> 11.9 us  [member_total(): return jnp.sum(lax.all_gather(partial_value, 'mem'), axis=0)]
where the time goes in v1:
time: 881 us; the launch traced here: 873 us
  blocking collectives  388 us (44%)
  waiting for transfers between devices  197 us (22%)
  local copies, waits for them, and re-layouts  122 us (14%)
  other arithmetic  85.5 us (10%)
  matrix products  50.7 us (6%)
  between operations  18.6 us (2%)
  starting transfers between devices  11.1 us (1%)
    all_to_all x2, blocking collectives, body(): lax.all_to_all(partial_value, 'lon', split_axis=2, concat_axis=1, tiled=T...  151 us
    all_gather x2, waiting for transfers between devices, member_total(): return jnp.sum(lax.all_gather(partial_value, 'mem'), axis=0)  127 us
    all_to_all x2, blocking collectives, adjoint_part(): lax.all_to_all(gridded, 'lon', split_axis=1, concat_axis=2, tiled=True)  118 us
    psum x2, blocking collectives, norm_total(): return lax.psum(jnp.sum(residual * residual), ('mem', 'lat', 'lon'))  79.9 us
    all_to_all x1, waiting for transfers between devices, adjoint_part(): lax.all_to_all(gridded, 'lon', split_axis=1, concat_axis=2, tiled=True)  49 us
    gather x2, local copies, waits for them, and re-layouts, body(): sampled = increment.reshape(-1)[located]  49 us
    scatter-add x3, other arithmetic, gridded_of(): jnp.zeros((levels * tile_rows * tile_cols,), jnp.float32).at[located]  38.4 us
    psum x1, blocking collectives, body(): curvature = lax.psum(jnp.sum(direction * image), ('mem', 'lat', 'lon'))  38.1 us
  transfers between devices with their start and end apart: 4, of which 4 were waited for; matrix products, arithmetic and copies ran while one was open for 4% of the time, Pallas kernels for 0%

profile of v1, /device:TPU:0, one launch (start us, length us, event | category | flops | bytes accessed | tf_op | source)
XLA Modules:
  0.0 873.0 jit_solution(2636380998650151632)
XLA Ops:
  8.6 12.8 %scatter_custom_fusion = f32[589824]{0:T(1024)} fusion(s32[2048]{0:T(1024)S(1)} %bitcast.74, f32[2048]{0:T(1024)S(1)} %mul.200, f32[]{:T(128)} %constant.20.clone.1), kind=kCustom, calls=%fused_computation.75 | custom fusion | flops 2048 | bytes 2359300 | tf_op jit(solution)/shard_map/scatter-add | solution.py:53
  29.4 6.3 all-to-all-start.1
  35.7 4.9 copy.43
  40.6 49.0 %all-to-all-done.1 = f32[4,384,384]{2,0,1:T(4,128)} async-done(((f32[4,384,384]{2,0,1:T(4,128)}), f32[4,384,384]{2,0,1:T(4,128)}, u32[]{:S(2)}, u32[]{:S(2)}) %all-to-all-start.1) | async-done | bytes 2359328 | tf_op jit(solution)/shard_map/all_to_all | solution.py:70
  94.5 5.9 fusion.18
  100.4 8.1 fusion.24
  108.5 6.8 fusion.21
  115.3 7.0 fusion.27
  125.9 21.6 %all-to-all-done = bf16[2,4,384,384]{3,1,0,2:T(4,128)(2,1)} async-done(((bf16[2,4,384,384]{3,1,0,2:T(4,128)(2,1)}), bf16[2,4,384,384]{3,1,0,2:T(4,128)(2,1)}, u32[]{:S(2)}, u32[]{:S(2)}) %all-to-all-start) | async-done | bytes 2359328 | tf_op jit(solution)/shard_map/all_to_all | solution.py:67
  147.6 5.7 copy.70
  153.3 6.4 reshape.141
  159.6 10.9 %fusion.47 = f32[2,4,96,512]{3,2,1,0:T(8,128)S(1)} fusion(f32[1536,256]{1,0:T(8,128)} %fusion.21, f32[1536,256]{1,0:T(8,128)S(1)} %fusion.18, f32[2,4,96,1536]{3,2,1,0:T(8,128)} %reshape.141, f32[4,96,1536]{2,1,0:T(8,128)} %bitcast.61, f32[4,512]{1,0:T(4,128)S(1)} %fusion.65), kind=kOutput, calls=%fused_computation.70 | convolution fusion | flops 7250903040 | bytes 11804672 | tf_op jit(solution)/shard_map/dot_general | solution.py:57
  170.6 10.3 %multiply_reduce_fusion.1 = f32[4,96,1536]{2,1,0:T(8,128)} fusion(f32[2,4,96,1536]{3,2,1,0:T(8,128)S(1)} %copy-done, f32[256,1536]{1,0:T(8,128)S(1)} %copy-done.10, f32[256,1536]{1,0:T(8,128)S(1)} %copy-done.8, f32[2,4,96,512]{3,2,1,0:T(8,128)S(1)} %fusion.47, f32[4,512]{1,0:T(4,128)S(1)} %fusion.65), kind=kOutput, calls=%fused_computation.11 | convolution fusion | flops 7251492864 | bytes 11804672 | tf_op jit(solution)/shard_map/dot_general | solution.py:81
  185.4 75.5 %all_to_all.84 = f32[4,96,1536]{1,0,2:T(4,128)} all-to-all(f32[4,96,1536]{1,0,2:T(4,128)} %copy.48), channel_id=1, replica_groups=mesh['mem'=4,'lat'=2,'lon'=4] {'lon'}, dimensions={2} | all-to-all | bytes 4718592 | tf_op jit(solution)/shard_map/all_to_all | solution.py:89
  261.0 4.7 copy.50
  265.7 63.4 %all-gather.3.cloned.1.call-done = f32[4,4,384,384]{3,2,1,0:T(8,128)} async-done(((f32[1,4,384,384]{3,2,1,0:T(8,128)}), f32[4,4,384,384]{3,2,1,0:T(8,128)}) %all-gather.3.cloned.1.call-update) | async-done | bytes 9437200 | tf_op jit(solution)/shard_map/all_gather | solution.py:36
  329.1 5.9 reduce_sum.74
  338.3 24.5 %gather_fusion = f32[2048]{0:T(1024)S(1)} fusion(f32[589824]{0:T(1024)} %reshape.137, s32[2048]{0:T(1024)S(1)} %broadcast_clamp_fusion), kind=kCustom, calls=%fused_computation | custom fusion | bytes 24576 | tf_op jit(solution)/shard_map/gather | solution.py:91
  362.8 12.8 %scatter_custom_fusion.1 = f32[589824]{0:T(1024)} fusion(s32[2048]{0:T(1024)S(1)} %bitcast.76, f32[2048]{0:T(1024)S(1)} %mul.226, f32[]{:T(128)} %constant.20.clone.1), kind=kCustom, calls=%fused_computation.73 | custom fusion | flops 2048 | bytes 2359300 | tf_op jit(solution)/shard_map/scatter-add | solution.py:53
  382.2 59.3 %all_to_all.85 = f32[4,384,384]{2,0,1:T(4,128)S(1)} all-to-all(f32[4,384,384]{2,0,1:T(4,128)S(1)} %copy.51), channel_id=1, replica_groups=mesh['mem'=4,'lat'=2,'lon'=4] {'lon'}, dimensions={1} | all-to-all | bytes 4718592 | tf_op jit(solution)/shard_map/all_to_all | solution.py:70
  443.7 8.6 multiply_reduce_fusion.4
  452.2 38.1 %all-reduce = (f32[]{:T(128)}, f32[]{:T(128)}) all-reduce(f32[]{:T(128)} %get-tuple-element.3, f32[]{:T(128)} %get-tuple-element.2), channel_id=1, replica_groups=mesh['mem'=4,'lat'=2,'lon'=4] {'mem','lat','lon'}, use_global_device_ids=true, to_apply=%region_2.3 | all-reduce | flops 2 | bytes 16 | tf_op jit(solution)/shard_map/psum | solution.py:40
  492.8 41.8 %psum.30 = f32[]{:T(128)} all-reduce(f32[]{:T(128)} %multiply_reduce_fusion.3), channel_id=1, replica_groups=mesh['mem'=4,'lat'=2,'lon'=4] {'mem','lat','lon'}, use_global_device_ids=true, to_apply=%region_9.10 | all-reduce | flops 1 | bytes 8 | tf_op jit(solution)/shard_map/psum | solution.py:40
  538.4 11.4 %multiply_reduce_fusion = f32[4,96,1536]{2,1,0:T(8,128)} fusion(f32[2,4,96,1536]{3,2,1,0:T(8,128)} %reshape.141, f32[256,1536]{1,0:T(8,128)S(1)} %copy-done.11, f32[256,1536]{1,0:T(8,128)S(1)} %copy-done.9, f32[2,4,96,512]{3,2,1,0:T(8,128)S(1)} %multiply_add_fusion.2, f32[4,512]{1,0:T(4,128)S(1)} %fusion.65), kind=kOutput, calls=%fused_computation.8 | convolution fusion | flops 7251492864 | bytes 11804672 | tf_op jit(solution)/shard_map/dot_general | solution.py:81
  554.3 75.7 %all_to_all.86 = f32[4,96,1536]{1,0,2:T(4,128)} all-to-all(f32[4,96,1536]{1,0,2:T(4,128)} %copy.54), channel_id=1, replica_groups=mesh['mem'=4,'lat'=2,'lon'=4] {'lon'}, dimensions={2} | all-to-all | bytes 4718592 | tf_op jit(solution)/shard_map/all_to_all | solution.py:89
  634.6 63.3 %all-gather.5.cloned.1.call-done = f32[4,4,384,384]{3,2,1,0:T(8,128)} async-done(((f32[1,4,384,384]{3,2,1,0:T(8,128)}), f32[4,4,384,384]{3,2,1,0:T(8,128)}) %all-gather.5.cloned.1.call-update) | async-done | bytes 9437200 | tf_op jit(solution)/shard_map/all_gather | solution.py:36
  697.9 6.0 reduce_sum.78
  707.1 24.5 %gather_fusion.1 = f32[2048]{0:T(1024)S(1)} fusion(f32[589824]{0:T(1024)} %reshape.139, s32[2048]{0:T(1024)S(1)} %broadcast_clamp_fusion), kind=kCustom, calls=%fused_computation.1 | custom fusion | bytes 24576 | tf_op jit(solution)/shard_map/gather | solution.py:91
  731.6 12.8 %scatter_custom_fusion.2 = f32[589824]{0:T(1024)} fusion(s32[2048]{0:T(1024)S(1)} %bitcast.77, f32[2048]{0:T(1024)S(1)} %mul.240, f32[]{:T(128)} %constant.20.clone.1), kind=kCustom, calls=%fused_computation.71 | custom fusion | flops 2048 | bytes 2359300 | tf_op jit(solution)/shard_map/scatter-add | solution.py:53
  751.0 59.1 %all_to_all.87 = f32[4,384,384]{2,0,1:T(4,128)S(1)} all-to-all(f32[4,384,384]{2,0,1:T(4,128)S(1)} %copy.57), channel_id=1, replica_groups=mesh['mem'=4,'lat'=2,'lon'=4] {'lon'}, dimensions={1} | all-to-all | bytes 4718592 | tf_op jit(solution)/shard_map/all_to_all | solution.py:70
  812.7 9.5 %multiply_reduce_fusion.2 = (f32[]{:T(128)}, f32[2,4,96,512]{3,2,1,0:T(8,128)}) fusion(f32[2,4,96,512]{3,2,1,0:T(8,128)S(1)} %copy-done.7, f32[4,512]{1,0:T(4,128)S(1)} %fusion.65, f32[1536,256]{1,0:T(8,128)S(1)} %copy-done.5, f32[1536,256]{1,0:T(8,128)S(1)} %copy-done.3, f32[2,4,96,1536]{3,2,1,0:T(8,128)S(1)} %bitcast.59, f32[4,96,1536]{2,1,0:T(8,128)S(1)} %bitcast.62), kind=kOutput, calls=%fused_computation.39 | convolution fusion | flops 7252082688 | bytes 13377540 | tf_op jit(solution)/shard_map/dot_general | solution.py:57
  822.2 38.1 %psum.31 = f32[]{:T(128)} all-reduce(f32[]{:T(128)} %get-tuple-element.9), channel_id=1, replica_groups=mesh['mem'=4,'lat'=2,'lon'=4] {'mem','lat','lon'}, use_global_device_ids=true, to_apply=%region_14.15 | all-reduce | flops 1 | bytes 8 | tf_op jit(solution)/shard_map/psum | solution.py:93
  (74 shorter events, 63.6 us)
Async XLA Ops:
  29.4 60.3 %all-to-all-start.1 = ((f32[4,384,384]{2,0,1:T(4,128)}), f32[4,384,384]{2,0,1:T(4,128)}, u32[]{:S(2)}, u32[]{:S(2)}) async-start(f32[4,384,384]{2,0,1:T(4,128)} %copy.45), calls=%async_computation.1 | async-start | bytes 4718592 | tf_op jit(solution)/shard_map/all_to_all | solution.py:70
  40.6 53.8 %copy-start.13 = (s32[4]{0:T(128)S(1)}, s32[4]{0:T(128)}, u32[]{:S(2)}) copy-start(s32[4]{0:T(128)} %param.11) | copy-start | bytes 52
  89.6 57.9 %all-to-all-start = ((bf16[2,4,384,384]{3,1,0,2:T(4,128)(2,1)}), bf16[2,4,384,384]{3,1,0,2:T(4,128)(2,1)}, u32[]{:S(2)}, u32[]{:S(2)}) async-start(bf16[2,4,384,384]{3,1,0,2:T(4,128)(2,1)} %copy.43), calls=%async_computation | async-start | bytes 4718592 | tf_op jit(solution)/shard_map/all_to_all | solution.py:67
  94.1 235.0 %all-gather.3.cloned.1.call-start = ((), (), s32[]{:S(2)}) async-start(), calls=%async_computation.6 | async-start | bytes 11796480 | tf_op jit(solution)/shard_map/all_gather | solution.py:36
  100.4 59.2 %copy-start.1 = (f32[1536,256]{1,0:T(8,128)}, f32[1536,256]{1,0:T(8,128)S(1)}, u32[]{:S(2)}) copy-start(f32[1536,256]{1,0:T(8,128)S(1)} %fusion.18) | copy-start | bytes 4718596
  159.6 10.9 %copy-start = (f32[2,4,96,1536]{3,2,1,0:T(8,128)S(1)}, f32[2,4,96,1536]{3,2,1,0:T(8,128)}, u32[]{:S(2)}) copy-start(f32[2,4,96,1536]{3,2,1,0:T(8,128)} %reshape.141) | copy-start | bytes 14155780
  159.6 10.9 %copy-start.8 = (f32[256,1536]{1,0:T(8,128)S(1)}, f32[256,1536]{1,0:T(8,128)}, u32[]{:S(2)}) copy-start(f32[256,1536]{1,0:T(8,128)} %fusion.24) | copy-start | bytes 4718596
  159.6 11.0 %copy-start.10 = (f32[256,1536]{1,0:T(8,128)S(1)}, f32[256,1536]{1,0:T(8,128)}, u32[]{:S(2)}) copy-start(f32[256,1536]{1,0:T(8,128)} %fusion.27) | copy-start | bytes 4718596
  265.7 432.3 %all-gather.5.cloned.1.call-start = ((), (), s32[]{:S(2)}) async-start(), calls=%async_computation.7 | async-start | bytes 11796480 | tf_op jit(solution)/shard_map/all_gather | solution.py:36
  338.3 24.5 %copy-start.12 = (f32[1,2048]{1,0:T(1,128)S(1)}, f32[1,2048]{1,0:T(1,128)}, u32[]{:S(2)}) copy-start(f32[1,2048]{1,0:T(1,128)} %param.8) | copy-start | bytes 24580
  382.2 59.9 %slice-start = ((s8[4718592]{0:T(1024)(128)(4,1)}), s8[4194304]{0:T(1024)(128)(4,1)S(1)}, s32[]{:S(2)}) async-start(s8[4718592]{0:T(1024)(128)(4,1)} %bitcast.56), calls=%async_computation.8 | async-start | bytes 8388608
  441.6 1.0 slice-start.1
  441.7 1.4 copy-start.2
  441.8 1.9 copy-start.4
  536.0 1.6 copy-start.9
  536.0 2.4 copy-start.11
  536.4 1.2 copy-start.6
  751.0 59.6 %slice-start.2 = ((s8[4718592]{0:T(1024)(128)(4,1)}), s8[4194304]{0:T(1024)(128)(4,1)S(1)}, s32[]{:S(2)}) async-start(s8[4718592]{0:T(1024)(128)(4,1)} %bitcast.58), calls=%async_computation.10 | async-start | bytes 8388608
  810.1 1.0 slice-start.3
  810.3 1.4 copy-start.3
  810.3 1.9 copy-start.5
  810.3 2.4 copy-start.7
Sparse Core Ops, SparseCore 0:
  265.8 63.3 all-gather.2
  634.7 63.1 all-gather.4
